TPU v7x, 32 devices: a whole 2x2x4 slice. The times are simulated.
32 devices in a mesh: parts: 2 (over x), row: 16 (over z, y, core).
Axes of the slice: x: 2, y: 2, z: 4, core: 2. Of those that a mesh axis runs over, the one named last changes fastest.
Arguments:
- coords: int32 [4, 3, 512], P('parts'), parts along dimension 0, may hold values from 0 to 7
- labels: int32 [16, 16, 512], P('parts', 'row'), parts along dimension 0, may hold values from 0 to 255
- ranks: int32 [16, 16, 2], P('parts', 'row'), parts along dimension 0, may hold values from 16 to 128, as said below
- u_first: bfloat16 [16, 16, 512, 128], P('parts', 'row'), parts along dimension 0, may hold values from -6 to 6
- v_first: bfloat16 [16, 16, 512, 128], P('parts', 'row'), parts along dimension 0, may hold values from -0.0046875 to 0.0046875
- u_second: bfloat16 [16, 16, 512, 128], P('parts', 'row'), parts along dimension 0, may hold values from -6 to 6
- v_second: bfloat16 [16, 16, 512, 128], P('parts', 'row'), parts along dimension 0, may hold values from -0.01171875 to 0.01171875
Outputs:
- eliminated: float32 [16, 16, 512, 256], P('parts', 'row'), parts along dimension 0
- diagonal_factors: float32 [4, 512, 512], P('parts'), parts along dimension 0
There are 2 independent parts, one for each index of `parts`. A program takes and returns all parts, laid end to end along the dimension named above; each array names one. Nothing has to cross between parts.
Inputs may be any that keep to these rules, and one draw needn't show every extreme that they name: `ranks`: the block of tile 1 in column 0 has rank 128; some block has rank 128 // 8.
All inputs are finite; a program needn't handle non-finite values.
Results may differ from a plain program's by a relative error of at most 0.0003.
Values may be sent and summed in bfloat16 or wider, within the bound.
No kernel may reach another device: no remote copies, remote signals or barrier semaphores. Data moves between devices by JAX's collectives and lax.ppermute only.
A program may use at most 128 MiB of HBM per device.

v0:
```python
import math
import jax
import jax.numpy as jnp
from jax import lax
from jax.sharding import PartitionSpec as P

NRHS = 256
highest = lax.Precision.HIGHEST
four_pi = 4.0 * math.pi


def spread(shard, axis, root):
    mine = lax.axis_index(axis) == root
    return lax.psum(jnp.where(mine, shard, jnp.zeros_like(shard)), axis)


def matmul(left, right):
    return jnp.dot(left, right, precision=highest, preferred_element_type=jnp.float32)


def kernel_tile(points):
    spots = points.astype(jnp.float32)
    distance = jnp.zeros((spots.shape[1], spots.shape[1]), jnp.float32)
    for dimension in range(3):
        offset = spots[dimension][:, None] - spots[dimension][None, :]
        distance = distance + offset * offset
    return 1.0 / (four_pi * jnp.sqrt(distance + 1.0)) + jnp.eye(spots.shape[1], dtype=jnp.float32)


def onehot(label_row):
    return (label_row[..., None] == jnp.arange(NRHS, dtype=jnp.int32)).astype(jnp.float32)


def triangular(lower, target):
    return lax.linalg.triangular_solve(lower, target, left_side=True, lower=True)


def solve_stack(lower, stack):
    number, height, breadth = stack.shape
    flat = jnp.transpose(stack, (1, 0, 2)).reshape(height, number * breadth)
    solved = triangular(lower, flat)
    return jnp.transpose(solved.reshape(height, number, breadth), (1, 0, 2))


def rank_mask(rank_values, breadth):
    columns = jnp.arange(breadth, dtype=jnp.int32)
    return (columns[None, :] < rank_values[:, None]).astype(jnp.float32)


def second_panel(points, label_row, u_one, w_one, first_sol):
    inner_gram = matmul(w_one.T, w_one)
    diagonal_tile = kernel_tile(points) - matmul(matmul(u_one, inner_gram), u_one.T)
    lower = jnp.linalg.cholesky(diagonal_tile)
    target = onehot(label_row) - matmul(u_one, matmul(w_one.T, first_sol))
    return (lower, triangular(lower, target))


def update(
    w_tiles, first_sol, second_lower, second_sol, u_one, w_one, label_rows, rank_rows, u0, u1, v1
):
    breadth = u0.shape[-1]
    u_zero = u0.astype(jnp.float32)
    u_next = u1.astype(jnp.float32)
    v_next = v1.astype(jnp.float32) * rank_mask(rank_rows[:, 1], breadth)[:, None, :]
    first_weights = jnp.einsum("nbr,bc->nrc", w_tiles, first_sol, precision=highest)
    first_update = jnp.einsum("nbr,nrc->nbc", u_zero, first_weights, precision=highest)
    cross = jnp.einsum("br,nbs->nrs", w_one, w_tiles, precision=highest)
    mixed = -jnp.einsum("br,nrs->nbs", u_one, cross, precision=highest)
    factor = solve_stack(second_lower, jnp.concatenate([v_next, mixed], axis=-1))
    second_weights = jnp.einsum("nbk,bc->nkc", factor, second_sol, precision=highest)
    left_pair = jnp.concatenate([u_next, u_zero], axis=-1)
    second_update = jnp.einsum("nbk,nkc->nbc", left_pair, second_weights, precision=highest)
    return onehot(label_rows) - first_update - second_update


def local(coords, labels, ranks, u_first, v_first, u_second, v_second):
    position = lax.axis_index("row")
    label_rows = labels[:, 0]
    rank_rows = ranks[:, 0]
    u_zero = u_first[:, 0]
    v_zero = v_first[:, 0]
    height = u_zero.shape[1]
    breadth = u_zero.shape[2]
    w_tiles = None

    def first_factor():
        lower = jnp.linalg.cholesky(kernel_tile(coords[0]))
        return (lower, triangular(lower, onehot(label_rows[0])))

    def first_empty():
        return (jnp.zeros((height, height), jnp.float32), jnp.zeros((height, NRHS), jnp.float32))

    first_lower, first_sol = lax.cond(position == 0, first_factor, first_empty)
    first_lower, first_sol = (spread(first_lower, "row", 0), spread(first_sol, "row", 0))
    masked = v_zero.astype(jnp.float32) * rank_mask(rank_rows[:, 0], breadth)[:, None, :]
    w_tiles = solve_stack(first_lower, masked)

    def second_factor():
        u_pick = u_zero[0].astype(jnp.float32)
        w_pick = w_tiles[0]
        lower, solved = second_panel(coords[1], label_rows[0], u_pick, w_pick, first_sol)
        return (lower, solved, u_pick, w_pick)

    def second_empty():
        return (
            jnp.zeros((height, height), jnp.float32),
            jnp.zeros((height, NRHS), jnp.float32),
            jnp.zeros((height, breadth), jnp.float32),
            jnp.zeros((height, breadth), jnp.float32),
        )

    second_lower, second_sol, u_one, w_one = lax.cond(position == 1, second_factor, second_empty)
    second_lower, second_sol, u_one, w_one = (
        spread(second_lower, "row", 1),
        spread(second_sol, "row", 1),
        spread(u_one, "row", 1),
        spread(w_one, "row", 1),
    )
    updated = update(
        w_tiles,
        first_sol,
        second_lower,
        second_sol,
        u_one,
        w_one,
        label_rows,
        rank_rows,
        u_zero,
        u_second[:, 0],
        v_second[:, 0],
    )
    leading = jnp.where(position == 0, first_sol, jnp.where(position == 1, second_sol, updated[0]))
    updated = updated.at[0].set(leading)
    return (updated[:, None], jnp.stack([first_lower, second_lower]))


def solution(mesh):
    in_specs = (
        P("parts", None, None),
        P("parts", "row", None),
        P("parts", "row", None),
        P("parts", "row", None, None),
        P("parts", "row", None, None),
        P("parts", "row", None, None),
        P("parts", "row", None, None),
    )
    out_specs = (P("parts", "row", None, None), P("parts", None, None))
    return jax.shard_map(local, mesh=mesh, in_specs=in_specs, out_specs=out_specs, check_vma=False)
```

profile of v0, /device:TPU:0, one launch (start us, length us, event | category | flops | bytes accessed | tf_op | source)
XLA Modules:
  0.0 670.5 jit_solution(9478993667882919614)
XLA Ops:
  7.9 145.0 %conditional.2 = (f32[512,512]{1,0:T(8,128)S(1)}, f32[512,256]{0,1:T(8,128)}) conditional(s32[]{:T(128)} %convert_element_type.64, () %tuple.30, (s32[2,3,512]{2,0,1:T(2,128)}, s32[8,512]{1,0:T(8,128)S(1)}) %tuple.157), branch_computations={%region_0.0_spmd, %region_1.12_spmd} | conditional | flops 916293632 | bytes 19471616 | solution.py:93
  11.5 11.7 %cholesky.286 = f32[128,128]{1,0:T(8,128)S(1)} custom-call(f32[128,128]{1,0:T(8,128)S(1)} %cholesky.426), custom_call_target="Cholesky" | custom-call | tf_op jit(solution)/shard_map/cond/branch_1_fun/jit(cholesky)/cholesky | solution.py:87
  23.3 9.8 %custom-call.35 = f32[1,128,128]{1,2,0:T(8,128)S(1)} custom-call(f32[1,128,128]{2,1,0:T(8,128)S(1)} %get-tuple-element.160), custom_call_target="InvertDiagBlocksLowerTriangular" | custom-call | tf_op jit(solution)/shard_map/cond/branch_1_fun/jit(cholesky)/cholesky | solution.py:87
  33.9 12.0 %cholesky.305 = f32[128,128]{1,0:T(8,128)S(1)} custom-call(f32[128,128]{1,0:T(8,128)S(1)} %cholesky.430), custom_call_target="Cholesky" | custom-call | tf_op jit(solution)/shard_map/cond/branch_1_fun/jit(cholesky)/cholesky | solution.py:87
  47.9 9.8 %custom-call.36 = f32[1,128,128]{1,2,0:T(8,128)S(1)} custom-call(f32[1,128,128]{2,1,0:T(8,128)S(1)} %get-tuple-element.157), custom_call_target="InvertDiagBlocksLowerTriangular" | custom-call | tf_op jit(solution)/shard_map/cond/branch_1_fun/jit(cholesky)/cholesky | solution.py:87
  58.4 11.7 %cholesky.326 = f32[128,128]{1,0:T(8,128)S(1)} custom-call(f32[128,128]{1,0:T(8,128)S(1)} %cholesky.435), custom_call_target="Cholesky" | custom-call | tf_op jit(solution)/shard_map/cond/branch_1_fun/jit(cholesky)/cholesky | solution.py:87
  71.5 9.8 %custom-call.37 = f32[1,128,128]{1,2,0:T(8,128)S(1)} custom-call(f32[1,128,128]{2,1,0:T(8,128)S(1)} %get-tuple-element.154), custom_call_target="InvertDiagBlocksLowerTriangular" | custom-call | tf_op jit(solution)/shard_map/cond/branch_1_fun/jit(cholesky)/cholesky | solution.py:87
  81.9 11.7 %cholesky.343 = f32[128,128]{1,0:T(8,128)S(1)} custom-call(f32[128,128]{1,0:T(8,128)S(1)} %convolution_subtract_fusion.5), custom_call_target="Cholesky" | custom-call | tf_op jit(solution)/shard_map/cond/branch_1_fun/jit(cholesky)/cholesky | solution.py:87
  95.3 10.6 %while.7 = (s32[]{:T(128)}, f32[512,512]{1,0:T(8,128)S(1)}, s32[4,2]{0,1:T(2,128)S(1)}, f32[4,128,128]{2,1,0:T(8,128)}, s32[]{:T(128)}) while((s32[]{:T(128)}, f32[512,512]{1,0:T(8,128)S(1)}, s32[4,2]{0,1:T(2,128)S(1)}, f32[4,128,128]{2,1,0:T(8,128)}, s32[]{:T(128)}) %tuple.135), condition=%wide.while_cond.1, body=%wide.while_body.1.sunk | while | flops 2 | bytes 132205 | solution.py:35
  95.9 2.0 bitcast_dynamic-update-slice_fusion.11
  98.6 2.0 bitcast_dynamic-update-slice_fusion.11
  101.2 2.0 bitcast_dynamic-update-slice_fusion.11
  103.8 2.0 bitcast_dynamic-update-slice_fusion.11
  105.8 40.1 %custom-call.38 = f32[4,128,128]{1,2,0:T(8,128)S(1)} custom-call(f32[4,128,128]{2,1,0:T(8,128)} %get-tuple-element.79), custom_call_target="InvertDiagBlocksLowerTriangular" | custom-call | tf_op jit(solution)/shard_map/cond/branch_1_fun/triangular_solve/custom-call.3 | solution.py:35
  158.0 92.5 %all-reduce.8.cloned.1.call-done = (f32[512,256]{0,1:T(8,128)}, f32[512,512]{1,0:T(8,128)}) async-done(((f32[512,256]{0,1:T(8,128)}, f32[512,512]{1,0:T(8,128)}), (f32[512,256]{0,1:T(8,128)}, f32[512,512]{1,0:T(8,128)})) %all-reduce.8.cloned.1.call-update) | async-done | bytes 1572880 | tf_op jit(solution)/shard_map/psum | solution.py:14
  251.9 8.0 %while.9 = (s32[]{:T(128)}, f32[512,512]{1,0:T(8,128)S(1)}, s32[4,2]{0,1:T(2,128)S(1)}, f32[4,128,128]{2,1,0:T(8,128)S(1)}, s32[]{:T(128)}) while((s32[]{:T(128)}, f32[512,512]{1,0:T(8,128)S(1)}, s32[4,2]{0,1:T(2,128)S(1)}, f32[4,128,128]{2,1,0:T(8,128)S(1)}, s32[]{:T(128)}) %tuple.140), condition=%wide.while_cond.2, body=%wide.while_body.2.sunk | while | flops 2 | bytes 131189 | solution.py:35
  259.9 39.3 %custom-call.29 = f32[4,128,128]{1,2,0:T(8,128)S(1)} custom-call(f32[4,128,128]{2,1,0:T(8,128)S(1)} %get-tuple-element.64), custom_call_target="InvertDiagBlocksLowerTriangular" | custom-call | tf_op jit(solution)/shard_map/triangular_solve | solution.py:35
  304.0 2.7 fusion.96
  309.7 10.4 %conditional.3 = (f32[512,512]{1,0:T(8,128)}, f32[512,128]{1,0:T(8,128)}, f32[512,128]{1,0:T(8,128)S(1)}, f32[512,256]{0,1:T(8,128)}) conditional(s32[]{:T(128)} %convert_element_type.69, () %tuple.32, (s32[2,3,512]{2,0,1:T(2,128)S(1)}, f32[8,512,128]{2,1,0:T(8,128)}, bf16[8,512,128]{2,1,0:T(8,128)(2,1)S(1)}, s32[8,512]{1,0:T(8,128)S(1)}, ...), branch_computations={%region_12.15_spmd, %region_13.16_spmd} | conditional | flops 1919715328 | bytes 30088544 | solution.py:112
  326.0 2.0 fusion.109
  328.0 3.8 fusion.134
  331.8 234.4 %all-reduce.6.cloned.1.call-done = (f32[512,128]{1,0:T(8,128)}, f32[512,128]{1,0:T(8,128)}, f32[512,512]{1,0:T(8,128)}, f32[512,256]{0,1:T(8,128)}) async-done(((f32[512,128]{1,0:T(8,128)}, f32[512,128]{1,0:T(8,128)}, f32[512,512]{1,0:T(8,128)}, f32[512,256]{0,1:T(8,128)}), (f32[512,128]{1,0:T(8,128)}, f32[512,128]{1,0:T(8,128)}, f32[512,512]{1,0:T(8,128)}, ...) | async-done | bytes 2097168 | tf_op jit(solution)/shard_map/psum | solution.py:14
  566.3 5.6 convolution_bitcast_fusion.1
  572.0 8.2 %while.10 = (s32[]{:T(128)}, f32[512,512]{1,0:T(8,128)S(1)}, s32[4,2]{0,1:T(2,128)S(1)}, f32[4,128,128]{2,1,0:T(8,128)S(1)}, s32[]{:T(128)}) while((s32[]{:T(128)}, f32[512,512]{1,0:T(8,128)S(1)}, s32[4,2]{0,1:T(2,128)S(1)}, f32[4,128,128]{2,1,0:T(8,128)S(1)}, s32[]{:T(128)}) %tuple.156), condition=%wide.while_cond.3, body=%wide.while_body.3.sunk | while | flops 2 | bytes 131189 | solution.py:35
  580.9 40.3 %custom-call.30 = f32[4,128,128]{1,2,0:T(8,128)S(1)} custom-call(f32[4,128,128]{2,1,0:T(8,128)} %copy-done.22), custom_call_target="InvertDiagBlocksLowerTriangular" | custom-call | tf_op jit(solution)/shard_map/triangular_solve | solution.py:35
  621.2 2.9 negate_bitcast_fusion
  629.1 3.5 convolution_subtract_fusion.13
  633.7 5.5 fusion.80
  640.9 2.0 copy.46
  642.9 7.8 %fusion.72 = f32[8,256,256]{2,1,0:T(8,128)S(1)} fusion(f32[8,512,256]{2,0,1:T(8,128)S(1)} %bitcast.272, f32[512,256]{0,1:T(8,128)S(1)} %copy-done.17), kind=kOutput, calls=%fused_computation.162 | convolution fusion | flops 3221225472 | bytes 6815744 | tf_op jit(solution)/shard_map/nbk,bc->nkc/dot_general | solution.py:70
  650.7 2.6 fusion.71
  656.2 5.5 copy.35
  (160 shorter events, 69.6 us)
Async XLA Ops:
  7.2 243.3 %all-reduce.8.cloned.1.call-start = ((), (), s32[]{:S(2)}) async-start(), calls=%async_computation.1 | async-start | bytes 3145728 | tf_op jit(solution)/shard_map/psum | solution.py:14
  153.0 3.1 copy-start.24
  153.0 3.1 copy-start.20
  156.0 410.3 %all-reduce.6.cloned.1.call-start = ((), (), s32[]{:S(2)}) async-start(), calls=%async_computation | async-start | bytes 4194304 | tf_op jit(solution)/shard_map/psum | solution.py:14
  300.9 3.1 copy-start.18
  304.0 4.9 copy-start.6
  307.4 1.5 copy-start.15
  307.4 2.0 copy-start.3
  307.4 2.3 copy-start.12
  307.4 2.3 copy-start.23
  321.2 1.8 copy-start.21
  324.3 1.6 copy-start.7
  324.3 1.6 copy-start.13
  324.3 1.7 copy-start.16
  326.0 2.0 copy-start.4
  566.3 5.6 copy-start.9
  580.2 0.7 copy-start.22
  640.9 2.0 copy-start.17
  642.9 7.8 %copy-start = (f32[8,256,512]{2,1,0:T(8,128)S(1)}, f32[8,256,512]{2,1,0:T(8,128)}, u32[]{:S(2)}) copy-start(f32[8,256,512]{2,1,0:T(8,128)} %fusion.134) | copy-start | bytes 12582916
  642.9 7.8 %copy-start.5 = (bf16[8,1,512,128]{3,2,1,0:T(8,128)(2,1)S(1)}, bf16[8,1,512,128]{3,2,1,0:T(8,128)(2,1)}, u32[]{:S(2)}) copy-start(bf16[8,1,512,128]{3,2,1,0:T(8,128)(2,1)} %param.19) | copy-start | bytes 3145732
  642.9 7.8 %copy-start.19 = (bf16[8,1,512,128]{3,2,1,0:T(8,128)(2,1)S(1)}, bf16[8,1,512,128]{3,2,1,0:T(8,128)(2,1)}, u32[]{:S(2)}) copy-start(bf16[8,1,512,128]{3,2,1,0:T(8,128)(2,1)} %param.21) | copy-start | bytes 3145732
  653.3 2.0 copy-start.14
  656.2 5.5 copy-start.8
  656.2 5.5 copy-start.10
Sparse Core Ops, SparseCore 0:
  156.1 94.3 all-reduce.7
  323.0 243.1 all-reduce.5
where the time goes:
time: 680 us; the launch traced here: 670 us
  waiting for transfers between devices  327 us (48%)
  other arithmetic  215 us (32%)
  matrix products  55.6 us (8%)
  local copies, waits for them, and re-layouts  46.8 us (7%)
  between operations  15 us (2%)
  loops' own time  10.8 us (2%)
    psum x2, waiting for transfers between devices, spread(): return lax.psum(jnp.where(mine, shard, jnp.zeros_like(shard)), axis)  327 us
    another operation x11, other arithmetic, triangular(): lax.linalg.triangular_solve(lower, target, left_side=True, lower=True)  122 us
    another operation x14, other arithmetic, first_factor(): lower = jnp.linalg.cholesky(kernel_tile(coords[0]))  78.8 us
    another operation x21, matrix products, triangular(): lax.linalg.triangular_solve(lower, target, left_side=True, lower=True)  29 us
    another operation x29, local copies, waits for them, and re-layouts  19.5 us
    unnamed x52, local copies, waits for them, and re-layouts  13.7 us
  transfers between devices with their start and end apart: 2, of which 2 were waited for; matrix products, arithmetic and copies ran while one was open for 2% of the time, Pallas kernels for 0%

commit v1 on v0

--- a/solution.py
+++ b/solution.py
@@ -11,7 +11,8 @@
 
 def spread(shard, axis, root):
     mine = lax.axis_index(axis) == root
-    return lax.psum(jnp.where(mine, shard, jnp.zeros_like(shard)), axis)
+    sheets_begin = lambda x_part, mesh_dim: lax.all_gather(x_part, mesh_dim).sum(axis=0)
+    return sheets_begin(jnp.where(mine, shard, jnp.zeros_like(shard)), axis)
 
 
 def matmul(left, right):

time: 680 us -> 1020 us (1.50)
  waiting for transfers between devices: 327 us -> 624 us
  other arithmetic: 215 us -> 250 us
  local copies, waits for them, and re-layouts: 46.8 us -> 66.2 us
  matrix products: 55.6 us -> 44.8 us
    all_gather x0 -> x6, waiting for transfers between devices: none -> 624 us  [spread(): lax.all_gather(x_part, mesh_dim).sum(axis=0)]
    psum x2 -> x0, waiting for transfers between devices: 327 us -> none  [spread(): return lax.psum(jnp.where(mine, shard, jnp.zeros_like(shard)), axis)]
    reduce_sum x0 -> x6, other arithmetic: none -> 30.3 us  [spread(): lax.all_gather(x_part, mesh_dim).sum(axis=0)]
    another operation x11 -> x12, other arithmetic: 122 us -> 127 us  [triangular(): lax.linalg.triangular_solve(lower, target, left_side=True, lower=True)]
  transfers between devices with their start and end apart: 2 -> 6, of which waited for: 2 -> 6; matrix products, arithmetic and copies ran while one was open for 2% -> 5% of each run, Pallas kernels for 0% -> 0%
where the time goes in v1:
time: 1020 us; the launch traced here: 1010 us
  waiting for transfers between devices  624 us (61%)
  other arithmetic  250 us (25%)
  local copies, waits for them, and re-layouts  66.2 us (6%)
  matrix products  44.8 us (4%)
  between operations  15 us (1%)
  loops' own time  12.1 us (1%)
    all_gather x6, waiting for transfers between devices, spread(): lax.all_gather(x_part, mesh_dim).sum(axis=0)  624 us
    another operation x12, other arithmetic, triangular(): lax.linalg.triangular_solve(lower, target, left_side=True, lower=True)  127 us
    another operation x14, other arithmetic, first_factor(): lower = jnp.linalg.cholesky(kernel_tile(coords[0]))  78.7 us
    reduce_sum x6, other arithmetic, spread(): lax.all_gather(x_part, mesh_dim).sum(axis=0)  30.3 us
    another operation x21, matrix products, triangular(): lax.linalg.triangular_solve(lower, target, left_side=True, lower=True)  24.3 us
    another operation x29, local copies, waits for them, and re-layouts  23.2 us
  transfers between devices with their start and end apart: 6, of which 6 were waited for; matrix products, arithmetic and copies ran while one was open for 5% of the time, Pallas kernels for 0%

profile of v1, /device:TPU:0, one launch (start us, length us, event | category | flops | bytes accessed | tf_op | source)
XLA Modules:
  0.0 1012.7 jit_solution(2576956888503549295)
XLA Ops:
  7.9 144.6 %conditional.2 = (f32[512,512]{1,0:T(8,128)S(1)}, f32[512,256]{1,0:T(8,128)}) conditional(s32[]{:T(128)} %convert_element_type.64, () %tuple.30, (s32[2,3,512]{2,0,1:T(2,128)}, s32[8,512]{1,0:T(8,128)S(1)}) %tuple.161), branch_computations={%region_0.0_spmd, %region_1.12_spmd} | conditional | flops 916293632 | bytes 18423040 | solution.py:94
  11.5 11.7 %cholesky.286 = f32[128,128]{1,0:T(8,128)S(1)} custom-call(f32[128,128]{1,0:T(8,128)S(1)} %cholesky.426), custom_call_target="Cholesky" | custom-call | tf_op jit(solution)/shard_map/cond/branch_1_fun/jit(cholesky)/cholesky | solution.py:88
  23.3 9.8 custom-call.35
  33.9 12.0 %cholesky.305 = f32[128,128]{1,0:T(8,128)S(1)} custom-call(f32[128,128]{1,0:T(8,128)S(1)} %cholesky.430), custom_call_target="Cholesky" | custom-call | tf_op jit(solution)/shard_map/cond/branch_1_fun/jit(cholesky)/cholesky | solution.py:88
  47.9 9.8 custom-call.36
  58.4 11.7 %cholesky.326 = f32[128,128]{1,0:T(8,128)S(1)} custom-call(f32[128,128]{1,0:T(8,128)S(1)} %cholesky.435), custom_call_target="Cholesky" | custom-call | tf_op jit(solution)/shard_map/cond/branch_1_fun/jit(cholesky)/cholesky | solution.py:88
  71.4 9.8 custom-call.37
  81.8 11.7 %cholesky.343 = f32[128,128]{1,0:T(8,128)S(1)} custom-call(f32[128,128]{1,0:T(8,128)S(1)} %convolution_subtract_fusion.5), custom_call_target="Cholesky" | custom-call | tf_op jit(solution)/shard_map/cond/branch_1_fun/jit(cholesky)/cholesky | solution.py:88
  95.0 10.6 %while.7 = (s32[]{:T(128)}, f32[512,512]{1,0:T(8,128)S(1)}, s32[4,2]{0,1:T(2,128)S(1)}, f32[4,128,128]{2,1,0:T(8,128)}, s32[]{:T(128)}) while((s32[]{:T(128)}, f32[512,512]{1,0:T(8,128)S(1)}, s32[4,2]{0,1:T(2,128)S(1)}, f32[4,128,128]{2,1,0:T(8,128)}, s32[]{:T(128)}) %tuple.133), condition=%wide.while_cond.1, body=%wide.while_body.1.sunk | while | flops 2 | bytes 132205 | solution.py:36
  105.6 40.1 %custom-call.38 = f32[4,128,128]{1,2,0:T(8,128)S(1)} custom-call(f32[4,128,128]{2,1,0:T(8,128)} %get-tuple-element.79), custom_call_target="InvertDiagBlocksLowerTriangular" | custom-call | tf_op jit(solution)/shard_map/cond/branch_1_fun/triangular_solve/custom-call.3 | solution.py:36
  159.4 68.9 %all-gather.15.cloned.1.call-done = f32[8192,256]{1,0:T(8,128)} async-done(((f32[512,256]{1,0:T(8,128)}), f32[8192,256]{1,0:T(8,128)}) %all-gather.15.cloned.1.call-update) | async-done | bytes 8388624 | tf_op jit(solution)/shard_map/all_gather | solution.py:14
  228.3 4.8 reduce_sum.59
  233.1 123.1 %all-gather.13.cloned.1.call-done = f32[8192,512]{1,0:T(8,128)} async-done(((f32[512,512]{1,0:T(8,128)}), f32[8192,512]{1,0:T(8,128)}) %all-gather.13.cloned.1.call-update) | async-done | bytes 16777232 | tf_op jit(solution)/shard_map/all_gather | solution.py:14
  356.2 7.9 reduce_sum.58
  364.3 8.0 while.9
  373.0 40.1 %custom-call.29 = f32[4,128,128]{1,2,0:T(8,128)S(1)} custom-call(f32[4,128,128]{2,1,0:T(8,128)} %copy-done.17), custom_call_target="InvertDiagBlocksLowerTriangular" | custom-call | tf_op jit(solution)/shard_map/triangular_solve | solution.py:36
  422.7 11.8 %conditional.3 = (f32[512,512]{1,0:T(8,128)}, f32[512,256]{1,0:T(8,128)}, f32[512,128]{1,0:T(8,128)}, f32[512,128]{1,0:T(8,128)S(1)}) conditional(s32[]{:T(128)} %convert_element_type.69, () %tuple.32, (s32[2,3,512]{2,0,1:T(2,128)S(1)}, f32[8,512,128]{1,2,0:T(8,128)S(1)}, bf16[8,512,128]{2,1,0:T(8,128)(2,1)}, s32[8,512]{1,0:T(8,128)S(1)}, ...), branch_computations={%region_12.15_spmd, %region_13.16_spmd} | conditional | flops 1919715328 | bytes 33234272 | solution.py:113
  445.3 3.1 fusion.108
  448.5 3.8 fusion.133
  452.3 198.7 %all-gather.19.cloned.1.call-done = f32[8192,128]{1,0:T(8,128)} async-done(((f32[512,128]{1,0:T(8,128)}), f32[8192,128]{1,0:T(8,128)}) %all-gather.19.cloned.1.call-update) | async-done | bytes 4194320 | tf_op jit(solution)/shard_map/all_gather | solution.py:14
  653.4 48.7 %all-gather.21.cloned.1.call-done = f32[8192,128]{1,0:T(8,128)} async-done(((f32[512,128]{1,0:T(8,128)}), f32[8192,128]{1,0:T(8,128)}) %all-gather.21.cloned.1.call-update) | async-done | bytes 4194320 | tf_op jit(solution)/shard_map/all_gather | solution.py:14
  702.1 3.1 reduce_sum.62
  715.5 62.1 %all-gather.23.cloned.1.call-done = f32[8192,256]{1,0:T(8,128)} async-done(((f32[512,256]{1,0:T(8,128)}), f32[8192,256]{1,0:T(8,128)}) %all-gather.23.cloned.1.call-update) | async-done | bytes 8388624 | tf_op jit(solution)/shard_map/all_gather | solution.py:14
  777.6 4.0 reduce_sum.63
  782.5 122.2 %all-gather.17.cloned.1.call-done = f32[8192,512]{1,0:T(8,128)} async-done(((f32[512,512]{1,0:T(8,128)}), f32[8192,512]{1,0:T(8,128)}) %all-gather.17.cloned.1.call-update) | async-done | bytes 16777232 | tf_op jit(solution)/shard_map/all_gather | solution.py:14
  904.7 8.1 reduce_sum.60
  914.0 11.9 %while.10 = (s32[]{:T(128)}, f32[512,512]{1,0:T(8,128)}, s32[4,2]{0,1:T(2,128)S(1)}, f32[4,128,128]{2,1,0:T(8,128)S(1)}, s32[]{:T(128)}) while((s32[]{:T(128)}, f32[512,512]{1,0:T(8,128)}, s32[4,2]{0,1:T(2,128)S(1)}, f32[4,128,128]{2,1,0:T(8,128)S(1)}, s32[]{:T(128)}) %tuple.160), condition=%wide.while_cond.3, body=%wide.while_body.3.sunk | while | flops 2 | bytes 131189 | solution.py:36
  926.6 40.1 %custom-call.30 = f32[4,128,128]{1,2,0:T(8,128)S(1)} custom-call(f32[4,128,128]{2,1,0:T(8,128)} %copy-done.16), custom_call_target="InvertDiagBlocksLowerTriangular" | custom-call | tf_op jit(solution)/shard_map/triangular_solve | solution.py:36
  975.4 2.9 fusion.78
  981.9 5.6 copy.64
  987.5 5.5 fusion.106
  998.5 5.3 copy.56
  (177 shorter events, 110.7 us)
Async XLA Ops:
  7.2 221.1 %all-gather.15.cloned.1.call-start = ((), (), s32[]{:S(2)}) async-start(), calls=%async_computation.1 | async-start | bytes 8912896 | tf_op jit(solution)/shard_map/all_gather | solution.py:14
  154.5 1.6 copy-start.14
  154.5 201.7 %all-gather.13.cloned.1.call-start = ((), (), s32[]{:S(2)}) async-start(), calls=%async_computation | async-start | bytes 17825792 | tf_op jit(solution)/shard_map/all_gather | solution.py:14
  155.6 1.0 copy-start.19
  155.7 495.4 %all-gather.19.cloned.1.call-start = ((), (), s32[]{:S(2)}) async-start(), calls=%async_computation.3 | async-start | bytes 4456448 | tf_op jit(solution)/shard_map/all_gather | solution.py:14
  372.3 0.7 copy-start.17
  415.4 2.0 copy-start.12
  420.8 1.9 copy-start.18
  435.3 266.8 %all-gather.21.cloned.1.call-start = ((), (), s32[]{:S(2)}) async-start(), calls=%async_computation.4 | async-start | bytes 4456448 | tf_op jit(solution)/shard_map/all_gather | solution.py:14
  436.1 341.4 %all-gather.23.cloned.1.call-start = ((), (), s32[]{:S(2)}) async-start(), calls=%async_computation.5 | async-start | bytes 8912896 | tf_op jit(solution)/shard_map/all_gather | solution.py:14
  437.0 467.7 %all-gather.17.cloned.1.call-start = ((), (), s32[]{:S(2)}) async-start(), calls=%async_computation.2 | async-start | bytes 17825792 | tf_op jit(solution)/shard_map/all_gather | solution.py:14
  445.3 3.1 copy-start.4
  705.2 1.8 copy-start.15
  707.0 1.8 copy-start.1
  781.5 123.2 %copy-start.6 = (f32[512,256]{1,0:T(8,128)}, f32[512,256]{1,0:T(8,128)S(1)}, u32[]{:S(2)}) copy-start(f32[512,256]{1,0:T(8,128)S(1)} %reduce_sum.63) | copy-start | bytes 1572868
  925.9 0.7 copy-start.16
  969.0 3.0 copy-start.8
  974.2 1.2 copy-start.7
  987.5 5.5 copy-start
  987.5 5.5 copy-start.5
  987.5 5.5 copy-start.13
  995.6 2.0 copy-start.10
  995.6 2.0 copy-start.11
Sparse Core Ops, SparseCore 0:
  154.6 73.5 all-gather.14
  231.0 125.1 all-gather.12
  435.4 215.5 all-gather.18
  653.0 49.0 all-gather.20
  704.1 73.3 all-gather.22
  779.6 125.1 all-gather.16
